TPU v7x, 32 devices: a whole 2x2x4 slice. The times are simulated.
32 devices in a mesh: rows: 8 (over y, x, core), cols: 4 (over z).
Axes of the slice: x: 2, y: 2, z: 4, core: 2. Of those that a mesh axis runs over, the one named last changes fastest.
Arguments:
- irradiance_layers: bfloat16 [2, 2048, 16384], P(None, ('rows', 'cols')), may hold values from 0 to 2
- initial_heat_anomaly: float32 [2, 2048, 16384], P(None, 'rows', 'cols'), may hold values from -12 to 12
- drift_rate_eastward: float32 [2, 2048, 16384], P(None, 'rows', 'cols'), may hold values from 0.35 to 0.45
- drift_rate_northward: float32 [2, 2048, 16384], P(None, 'rows', 'cols'), may hold values from 0.33 to 0.4
- extinction_factor: float32 [2, 2048, 16384], P(None, 'rows', 'cols'), may hold values from 0.1 to 1
- windward_polarity_eastward: int32 [2, 2048], P(None, 'rows'), may hold values from 0 to 1
- windward_polarity_northward: int32 [2, 16384], P(None, 'cols'), may hold values from 0 to 1
Outputs:
- phase_slabs: float32 [2, 2048, 16384], P(None, ('rows', 'cols'))
- temperature_end: float32 [2, 2048, 16384], P(None, 'rows', 'cols')
Inputs may be any that keep to these rules, and one draw needn't show every extreme that they name: `windward_polarity_eastward`: 1 means wind plus slew toward increasing x. `windward_polarity_northward`: 1 means wind plus slew toward increasing y.
All inputs are finite; a program needn't handle non-finite values.
Results may differ from a plain program's by a relative error of at most 0.0003.
Values may be sent and summed in bfloat16 or wider, within the bound.
No kernel may reach another device: no remote copies, remote signals or barrier semaphores. Data moves between devices by JAX's collectives and lax.ppermute only.
A program may use at most 192 MiB of HBM per device.

v0:
```python
import jax
import jax.numpy as jnp
from jax import lax
from jax.sharding import PartitionSpec as P

SUBSTEPS = 4
DIFFUSION = 0.03
HEAT_RATE = 0.25


def extended(block, sides, width):
    for axis, dim in sides:
        count = lax.axis_size(axis)
        forward = [(i, i + 1) for i in range(count - 1)]
        backward = [(target, source) for source, target in forward]
        low = lax.ppermute(
            lax.slice_in_dim(block, block.shape[dim] - width, None, axis=dim), axis, forward
        )
        high = lax.ppermute(lax.slice_in_dim(block, 0, width, axis=dim), axis, backward)
        block = jnp.concatenate([low, block, high], axis=dim)
    return block


def advance(padded, wind_x, wind_y, heating):
    middle = padded[1:-1, 1:-1]
    west_cell = padded[1:-1, :-2]
    east_cell = padded[1:-1, 2:]
    south_cell = padded[:-2, 1:-1]
    north_cell = padded[2:, 1:-1]
    upwind_x = jnp.where(wind_x > 0, west_cell, east_cell)
    upwind_y = jnp.where(wind_y > 0, south_cell, north_cell)
    neighbours = west_cell + east_cell + south_cell + north_cell - 4.0 * middle
    return (
        middle
        - jnp.abs(wind_x) * (middle - upwind_x)
        - jnp.abs(wind_y) * (middle - upwind_y)
        + DIFFUSION * neighbours
        + heating
    )


def body(
    irradiance_layers,
    initial_heat_anomaly,
    drift_rate_eastward,
    drift_rate_northward,
    extinction_factor,
    windward_polarity_eastward,
    windward_polarity_northward,
):
    optical_layers = initial_heat_anomaly.shape[0]
    arrived = lax.all_to_all(irradiance_layers, "cols", split_axis=2, concat_axis=1, tiled=True)
    phases = []
    finals = []
    for optical_layer in range(optical_layers):
        light_tile = arrived[optical_layer]
        wind_x = jnp.where(
            windward_polarity_eastward[optical_layer][:, None] == 1,
            drift_rate_eastward[optical_layer],
            -drift_rate_eastward[optical_layer],
        )
        wind_y = jnp.where(
            windward_polarity_northward[optical_layer][None, :] == 1,
            drift_rate_northward[optical_layer],
            -drift_rate_northward[optical_layer],
        )
        heating = HEAT_RATE * extinction_factor[optical_layer] * light_tile.astype(jnp.float32)
        heat_transport_advance = initial_heat_anomaly[optical_layer]
        phase_sum = jnp.zeros_like(heat_transport_advance)
        for section_index in range(SUBSTEPS):
            padded = extended(heat_transport_advance, (("rows", 0), ("cols", 1)), 1)
            heat_transport_advance = advance(padded, wind_x, wind_y, heating)
            phase_sum = phase_sum + heat_transport_advance / SUBSTEPS
        phases.append(phase_sum)
        finals.append(heat_transport_advance)
    phase_slabs = lax.all_to_all(jnp.stack(phases), "cols", split_axis=1, concat_axis=2, tiled=True)
    return (phase_slabs, jnp.stack(finals))


def solution(mesh):
    return jax.shard_map(
        body,
        mesh=mesh,
        in_specs=(
            P(None, ("rows", "cols"), None),
            P(None, "rows", "cols"),
            P(None, "rows", "cols"),
            P(None, "rows", "cols"),
            P(None, "rows", "cols"),
            P(None, "rows"),
            P(None, "cols"),
        ),
        out_specs=(P(None, ("rows", "cols"), None), P(None, "rows", "cols")),
        check_vma=False,
    )
```

profile of v0, /device:TPU:3, one launch (start us, length us, event | category | flops | bytes accessed | tf_op | source)
XLA Modules:
  0.0 627.5 jit_solution(5142534280835631980)
XLA Ops:
  0.6 17.8 %copy.19 = bf16[2,64,16384]{1,0,2:T(2,128)(2,1)} copy(bf16[2,64,16384]{2,1,0:T(8,128)(2,1)} %param.7) | data formatting | bytes 8388608 | tf_op args[0]
  18.4 9.6 %reshape.44 = bf16[4,2,262144]{2,1,0:T(2,128)(2,1)} reshape(bf16[16384,2,64]{2,1,0:T(2,128)(2,1)} %bitcast.140) | data formatting | bytes 8388608
  28.0 5.0 all-to-all-start
  32.9 1.1 slice_bitcast_fusion.4
  34.1 3.7 collective-permute-start
  37.8 1.9 collective-permute-start.1
  39.7 4.5 collective-permute-start.16
  44.3 1.9 collective-permute-start.17
  46.3 4.0 slice_bitcast_fusion.1
  50.5 3.7 collective-permute-start.2
  54.2 1.3 collective-permute-start.3
  55.7 4.0 collective-permute-start.18
  59.7 1.3 collective-permute-start.19
  61.0 64.7 %all-to-all-done = bf16[4,2,262144]{2,1,0:T(2,128)(2,1)} async-done(((bf16[4,2,262144]{2,1,0:T(2,128)(2,1)}), bf16[4,2,262144]{2,1,0:T(2,128)(2,1)}, u32[]{:S(2)}, u32[]{:S(2)}) %all-to-all-start) | async-done | bytes 4194336 | tf_op jit(solution)/shard_map/all_to_all | solution.py:52
  125.6 9.3 %reshape.45 = bf16[16384,2,64]{2,1,0:T(2,128)(2,1)} reshape(bf16[4,2,262144]{2,1,0:T(2,128)(2,1)} %all-to-all-done) | data formatting | bytes 8388608
  134.9 18.6 %copy.21 = bf16[2,64,4,4096]{3,1,2,0:T(8,128)(2,1)} copy(bf16[2,64,4,4096]{1,0,3,2:T(2,128)(2,1)} %bitcast.139) | data formatting | bytes 8388608 | tf_op jit(solution)/shard_map/all_to_all | solution.py:52
  153.5 4.2 fusion.15
  158.4 20.0 %add_add_fusion.7 = (f32[256,4096]{1,0:T(8,128)S(1)}, pred[256,4096]{1,0:T(8,128)(4,1)}, pred[256,4096]{1,0:T(8,128)(4,1)}) fusion(f32[256,4096]{1,0:T(8,128)} %copy-done.8, f32[1,4096]{1,0:T(1,128)S(1)} %collective-permute-done, f32[1,4096]{1,0:T(1,128)S(1)} %collective-permute-done.1, f32[258,1]{1,0:T(8,128)} %copy-done.12, f32[258,1]{1,0:T(8,128)} %copy-done.13, ...), kind=kLoop, calls=%fused_computation.82 | loop fusion | flops 36700160 | bytes 25205008 | tf_op jit(solution)/shard_map/add | solution.py:34
  178.5 5.6 collective-permute-start.4
  184.1 1.9 collective-permute-start.5
  186.2 19.6 %add_add_fusion.3 = (f32[256,4096]{1,0:T(8,128)S(1)}, pred[256,4096]{1,0:T(8,128)(4,1)}, pred[256,4096]{1,0:T(8,128)(4,1)}) fusion(f32[256,4096]{1,0:T(8,128)} %copy-done.7, f32[1,4096]{1,0:T(1,128)S(1)} %collective-permute-done.16, f32[1,4096]{1,0:T(1,128)S(1)} %collective-permute-done.17, f32[258,1]{1,0:T(8,128)S(1)} %collective-permute-done.18, ...), kind=kLoop, calls=%fused_computation.76 | loop fusion | flops 36700160 | bytes 25205008 | tf_op jit(solution)/shard_map/add | solution.py:34
  205.8 4.5 collective-permute-start.20
  210.3 1.9 collective-permute-start.21
  212.4 1.3 collective-permute-start.6
  213.7 1.3 collective-permute-start.7
  215.0 1.3 collective-permute-done.21
  216.4 2.9 collective-permute-start.22
  219.3 1.3 collective-permute-start.23
  221.9 12.6 %add_add_fusion.6 = f32[256,4096]{1,0:T(8,128)} fusion(f32[256,4096]{1,0:T(8,128)S(1)} %get-tuple-element.8, pred[256,4096]{1,0:T(8,128)(4,1)} %get-tuple-element.10, f32[1,4096]{1,0:T(1,128)S(1)} %collective-permute-done.4, f32[1,4096]{1,0:T(1,128)S(1)} %collective-permute-done.5, pred[256,4096]{1,0:T(8,128)(4,1)} %get-tuple-element.9, ...), kind=kLoop, calls=%fused_computation.81 | loop fusion | flops 34603008 | bytes 25205008 | tf_op jit(solution)/shard_map/add | solution.py:34
  234.6 1.6 fusion.13
  236.2 5.1 collective-permute-start.8
  241.3 1.9 collective-permute-start.9
  243.2 18.1 %add_add_fusion.2 = f32[256,4096]{1,0:T(8,128)} fusion(f32[256,4096]{1,0:T(8,128)} %copy-done, pred[256,4096]{1,0:T(8,128)(4,1)} %get-tuple-element.15, f32[1,4096]{1,0:T(1,128)S(1)} %collective-permute-done.20, f32[1,4096]{1,0:T(1,128)} %copy-done.22, pred[256,4096]{1,0:T(8,128)(4,1)} %get-tuple-element.14, f32[258,1]{1,0:T(8,128)S(1)} %collective-permute-done.22, ...), kind=kLoop, calls=%fused_computation.75 | loop fusion | flops 34603008 | bytes 25205008 | tf_op jit(solution)/shard_map/add | solution.py:34
  261.3 1.1 fusion.17
  262.4 4.7 collective-permute-start.24
  267.1 1.9 collective-permute-start.25
  269.0 1.1 pad_maximum_fusion.81
  270.1 4.3 collective-permute-start.10
  274.4 1.3 collective-permute-start.11
  276.3 4.0 collective-permute-start.26
  280.3 1.5 collective-permute-start.27
  282.5 18.8 %add_add_fusion.5 = f32[256,4096]{1,0:T(8,128)} fusion(f32[256,4096]{1,0:T(8,128)} %add_add_fusion.6, pred[256,4096]{1,0:T(8,128)(4,1)} %get-tuple-element.10, f32[1,4096]{1,0:T(1,128)S(1)} %collective-permute-done.8, f32[1,4096]{1,0:T(1,128)S(1)} %collective-permute-done.9, pred[256,4096]{1,0:T(8,128)(4,1)} %get-tuple-element.9, f32[258,1]{1,0:T(8,128)} %copy-done.15, ...), kind=kLoop, calls=%fused_computation.80 | loop fusion | flops 34603008 | bytes 25205008 | tf_op jit(solution)/shard_map/add | solution.py:34
  301.3 1.6 fusion.12
  302.9 5.4 collective-permute-start.12
  308.3 1.9 collective-permute-start.13
  310.2 18.1 %add_add_fusion.1 = f32[256,4096]{1,0:T(8,128)} fusion(f32[256,4096]{1,0:T(8,128)} %add_add_fusion.2, pred[256,4096]{1,0:T(8,128)(4,1)} %get-tuple-element.15, f32[1,4096]{1,0:T(1,128)S(1)} %collective-permute-done.24, f32[1,4096]{1,0:T(1,128)} %copy-done.23, pred[256,4096]{1,0:T(8,128)(4,1)} %get-tuple-element.14, f32[258,1]{1,0:T(8,128)S(1)} %collective-permute-done.26, ...), kind=kLoop, calls=%fused_computation.74 | loop fusion | flops 34603008 | bytes 25205008 | tf_op jit(solution)/shard_map/add | solution.py:34
  329.3 4.5 collective-permute-start.28
  333.9 2.3 collective-permute-start.29
  336.3 1.1 pad_maximum_fusion.80
  337.4 4.3 collective-permute-start.14
  341.7 1.3 collective-permute-start.15
  343.1 1.8 pad_maximum_fusion.68
  344.8 4.8 collective-permute-start.30
  349.6 1.7 collective-permute-start.31
  351.4 20.9 %multiply_bitcast_fusion = (f32[1,256,4096]{2,1,0:T(8,128)}, f32[256,4096]{1,0:T(8,128)}) fusion(f32[256,4096]{1,0:T(8,128)} %add_add_fusion.5, f32[256,4096]{1,0:T(8,128)S(1)} %get-tuple-element.8, f32[256,4096]{1,0:T(8,128)S(1)} %copy-done.2, bf16[1,4,64,4096]{3,2,1,0:T(8,128)(2,1)S(1)} %copy-done.6, f32[2,256,4096]{2,1,0:T(8,128)} %param.11, ...), kind=kLoop, calls=%fused_computation.78 | loop fusion | flops 38797312 | bytes 37787920 | tf_op jit(solution)/shard_map/stack | solution.py:76
  372.3 8.7 %copy.22 = f32[1,256,4096]{2,0,1:T(1,128)} copy(f32[1,256,4096]{2,1,0:T(8,128)} %get-tuple-element.6) | data formatting | bytes 8388608 | tf_op jit(solution)/shard_map/stack | solution.py:76
  381.1 19.5 %add_multiply_fusion = (f32[256,4096]{1,0:T(8,128)S(1)}, f32[256,4096]{1,0:T(8,128)}) fusion(f32[256,4096]{1,0:T(8,128)} %add_add_fusion.1, f32[256,4096]{1,0:T(8,128)S(1)} %copy-done.1, f32[256,4096]{1,0:T(8,128)} %add_add_fusion.2, bf16[1,4,64,4096]{3,2,1,0:T(8,128)(2,1)S(1)} %copy-done.4, f32[2,256,4096]{2,1,0:T(8,128)} %param.11, ...), kind=kLoop, calls=%fused_computation.72 | loop fusion | flops 38797312 | bytes 37787920 | tf_op jit(solution)/shard_map/add | solution.py:73
  400.6 4.6 stack.19
  405.2 9.2 %pad_maximum_fusion = f32[2,256,4096]{2,0,1:T(2,128)} fusion(f32[1,256,4096]{2,0,1:T(1,128)S(1)} %stack.19, f32[1,256,4096]{2,0,1:T(1,128)S(1)} %copy-done.11), kind=kLoop, calls=%fused_computation | loop fusion | flops 2097152 | bytes 16777216 | tf_op jit(solution)/shard_map/stack | solution.py:76
  414.4 6.8 %all-to-all-start.1 = ((f32[2,256,4096]{2,0,1:T(2,128)}), f32[2,256,4096]{2,0,1:T(2,128)}, u32[]{:S(2)}, u32[]{:S(2)}) async-start(f32[2,256,4096]{2,0,1:T(2,128)} %pad_maximum_fusion), calls=%async_computation.1 | async-start | bytes 16777216 | tf_op jit(solution)/shard_map/all_to_all | solution.py:76
  421.2 7.9 %pad_maximum_fusion.1 = f32[2,256,4096]{2,1,0:T(8,128)} fusion(f32[1,256,4096]{2,1,0:T(8,128)} %bitcast.143, f32[1,256,4096]{2,1,0:T(8,128)} %bitcast.142), kind=kLoop, calls=%fused_computation.1 | loop fusion | flops 2097152 | bytes 16777216 | tf_op jit(solution)/shard_map/stack | solution.py:77
  429.0 175.3 %all-to-all-done.1 = f32[2,256,4096]{2,0,1:T(2,128)} async-done(((f32[2,256,4096]{2,0,1:T(2,128)}), f32[2,256,4096]{2,0,1:T(2,128)}, u32[]{:S(2)}, u32[]{:S(2)}) %all-to-all-start.1) | async-done | bytes 8388640 | tf_op jit(solution)/shard_map/all_to_all | solution.py:76
  604.3 12.1 %copy.23 = f32[2,64,4,4096]{3,2,1,0:T(4,128)} copy(f32[2,64,4,4096]{3,0,1,2:T(2,128)} %bitcast.18) | data formatting | bytes 16777216 | tf_op jit(solution)/shard_map/all_to_all | solution.py:76
  616.4 10.9 %all_to_all.30 = f32[2,64,16384]{2,1,0:T(8,128)} reshape(f32[2,64,4,4096]{3,2,1,0:T(4,128)} %copy.23) | data formatting | bytes 16777216 | tf_op jit(solution)/shard_map/all_to_all | solution.py:76
  (112 shorter events, 5.0 us)
Async XLA Ops:
  28.0 18.2 %copy-start.24 = (s32[2,4096]{1,0:T(2,128)S(1)}, s32[2,4096]{1,0:T(2,128)}, u32[]{:S(2)}) copy-start(s32[2,4096]{1,0:T(2,128)} %param.13) | copy-start | bytes 98308
  28.0 97.7 %all-to-all-start = ((bf16[4,2,262144]{2,1,0:T(2,128)(2,1)}), bf16[4,2,262144]{2,1,0:T(2,128)(2,1)}, u32[]{:S(2)}, u32[]{:S(2)}) async-start(bf16[4,2,262144]{2,1,0:T(2,128)(2,1)} %reshape.44), calls=%async_computation | async-start | bytes 8388608 | tf_op jit(solution)/shard_map/all_to_all | solution.py:52
  34.1 16.3 %collective-permute-start = (f32[1,4096]{1,0:T(1,128)S(1)}, f32[1,4096]{1,0:T(1,128)S(1)}, u32[]{:S(2)}, u32[]{:S(2)}) collective-permute-start(f32[1,4096]{1,0:T(1,128)S(1)} %get-tuple-element.17), channel_id=1, source_target_pairs={{0,4},{4,8},{8,12},{12,16},{16,20},{20,24},{24,28},{1,5},{5,9},{9,... | collective-permute-start | bytes 49160 | tf_op jit(solution)/shard_map/ppermute | solution.py:16
  37.8 12.6 %collective-permute-start.1 = (f32[1,4096]{1,0:T(1,128)S(1)}, f32[1,4096]{1,0:T(1,128)S(1)}, u32[]{:S(2)}, u32[]{:S(2)}) collective-permute-start(f32[1,4096]{1,0:T(1,128)S(1)} %get-tuple-element.16), channel_id=1, source_target_pairs={{4,0},{8,4},{12,8},{16,12},{20,16},{24,20},{28,24},{5,1},{9,5},{13... | collective-permute-start | bytes 49160 | tf_op jit(solution)/shard_map/ppermute | solution.py:19
  39.7 15.8 %collective-permute-start.16 = (f32[1,4096]{1,0:T(1,128)S(1)}, f32[1,4096]{1,0:T(1,128)S(1)}, u32[]{:S(2)}, u32[]{:S(2)}) collective-permute-start(f32[1,4096]{1,0:T(1,128)S(1)} %get-tuple-element.19), channel_id=1, source_target_pairs={{0,4},{4,8},{8,12},{12,16},{16,20},{20,24},{24,28},{1,5},{5,9},{9,... | collective-permute-start | bytes 49160 | tf_op jit(solution)/shard_map/ppermute | solution.py:16
  44.3 11.3 %collective-permute-start.17 = (f32[1,4096]{1,0:T(1,128)S(1)}, f32[1,4096]{1,0:T(1,128)S(1)}, u32[]{:S(2)}, u32[]{:S(2)}) collective-permute-start(f32[1,4096]{1,0:T(1,128)S(1)} %get-tuple-element.18), channel_id=1, source_target_pairs={{4,0},{8,4},{12,8},{16,12},{20,16},{24,20},{28,24},{5,1},{9,5},{13... | collective-permute-start | bytes 49160 | tf_op jit(solution)/shard_map/ppermute | solution.py:19
  46.3 4.0 copy-start.27
  50.4 5.3 copy-start.7
  50.4 5.3 copy-start.8
  50.4 232.1 %copy-start.25 = (pred[256]{0:T(512)(128)(4,1)}, pred[256]{0:T(512)(128)(4,1)S(1)}, u32[]{:S(2)}) copy-start(pred[256]{0:T(512)(128)(4,1)S(1)} %get-tuple-element.4) | copy-start | bytes 772
  50.5 107.2 %collective-permute-start.2 = (f32[258,1]{1,0:T(8,128)S(1)}, f32[258,1]{1,0:T(8,128)S(1)}, u32[]{:S(2)}, u32[]{:S(2)}) collective-permute-start(f32[258,1]{1,0:T(8,128)S(1)} %get-tuple-element.29), channel_id=1, source_target_pairs={{0,1},{1,2},{2,3},{4,5},{5,6},{6,7},{8,9},{9,10},{10,11},{12,13},{... | collective-permute-start | bytes 3104 | tf_op jit(solution)/shard_map/ppermute | solution.py:16
  54.2 103.5 %collective-permute-start.3 = (f32[258,1]{1,0:T(8,128)S(1)}, f32[258,1]{1,0:T(8,128)S(1)}, u32[]{:S(2)}, u32[]{:S(2)}) collective-permute-start(f32[258,1]{1,0:T(8,128)S(1)} %get-tuple-element.28), channel_id=1, source_target_pairs={{1,0},{2,1},{3,2},{5,4},{6,5},{7,6},{9,8},{10,9},{11,10},{13,12},{... | collective-permute-start | bytes 3104 | tf_op jit(solution)/shard_map/ppermute | solution.py:19
  55.7 130.4 %collective-permute-start.18 = (f32[258,1]{1,0:T(8,128)S(1)}, f32[258,1]{1,0:T(8,128)S(1)}, u32[]{:S(2)}, u32[]{:S(2)}) collective-permute-start(f32[258,1]{1,0:T(8,128)S(1)} %get-tuple-element.37), channel_id=1, source_target_pairs={{0,1},{1,2},{2,3},{4,5},{5,6},{6,7},{8,9},{9,10},{10,11},{12,13},{... | collective-permute-start | bytes 3104 | tf_op jit(solution)/shard_map/ppermute | solution.py:16
  59.7 126.4 %collective-permute-start.19 = (f32[258,1]{1,0:T(8,128)S(1)}, f32[258,1]{1,0:T(8,128)}, u32[]{:S(2)}, u32[]{:S(2)}) collective-permute-start(f32[258,1]{1,0:T(8,128)S(1)} %get-tuple-element.36), channel_id=1, source_target_pairs={{1,0},{2,1},{3,2},{5,4},{6,5},{7,6},{9,8},{10,9},{11,10},{13,12},{... | collective-permute-start | bytes 3104 | tf_op jit(solution)/shard_map/ppermute | solution.py:19
  153.5 32.6 %slice-start = ((s8[8388608]{0:T(1024)(128)(4,1)}), s8[4194304]{0:T(1024)(128)(4,1)S(1)}, s32[]{:S(2)}) async-start(s8[8388608]{0:T(1024)(128)(4,1)} %bitcast.133), calls=%async_computation.2 | async-start | bytes 8388608
  153.5 32.6 %slice-start.2 = ((s8[8388608]{0:T(1024)(128)(4,1)}), s8[4194304]{0:T(1024)(128)(4,1)S(1)}, s32[]{:S(2)}) async-start(s8[8388608]{0:T(1024)(128)(4,1)} %bitcast.135), calls=%async_computation.4 | async-start | bytes 8388608
  153.5 32.6 %slice-start.4 = ((s8[8388608]{0:T(1024)(128)(4,1)}), s8[4194304]{0:T(1024)(128)(4,1)S(1)}, s32[]{:S(2)}) async-start(s8[8388608]{0:T(1024)(128)(4,1)} %bitcast.137), calls=%async_computation.6 | async-start | bytes 8388608
  157.7 20.8 %copy-start.5 = (bf16[1,4,64,4096]{3,2,1,0:T(8,128)(2,1)}, bf16[1,4,64,4096]{3,2,1,0:T(8,128)(2,1)S(1)}, u32[]{:S(2)}) copy-start(bf16[1,4,64,4096]{3,2,1,0:T(8,128)(2,1)S(1)} %get-tuple-element.44) | copy-start | bytes 6291460
  157.7 0.7 copy-start.13
  158.4 27.7 %slice-start.1 = ((s8[8388608]{0:T(1024)(128)(4,1)}), s8[4194304]{0:T(1024)(128)(4,1)S(1)}, s32[]{:S(2)}) async-start(s8[8388608]{0:T(1024)(128)(4,1)} %bitcast.133), calls=%async_computation.3 | async-start | bytes 8388608
  158.4 27.7 %slice-start.3 = ((s8[8388608]{0:T(1024)(128)(4,1)}), s8[4194304]{0:T(1024)(128)(4,1)S(1)}, s32[]{:S(2)}) async-start(s8[8388608]{0:T(1024)(128)(4,1)} %bitcast.135), calls=%async_computation.5 | async-start | bytes 8388608
  158.4 27.7 %slice-start.5 = ((s8[8388608]{0:T(1024)(128)(4,1)}), s8[4194304]{0:T(1024)(128)(4,1)S(1)}, s32[]{:S(2)}) async-start(s8[8388608]{0:T(1024)(128)(4,1)} %bitcast.137), calls=%async_computation.7 | async-start | bytes 8388608
  178.5 33.7 %collective-permute-start.4 = (f32[1,4096]{1,0:T(1,128)S(1)}, f32[1,4096]{1,0:T(1,128)S(1)}, u32[]{:S(2)}, u32[]{:S(2)}) collective-permute-start(f32[1,4096]{1,0:T(1,128)S(1)} %get-tuple-element.43), channel_id=1, source_target_pairs={{0,4},{4,8},{8,12},{12,16},{16,20},{20,24},{24,28},{1,5},{5,9},{9,... | collective-permute-start | bytes 49160 | tf_op jit(solution)/shard_map/ppermute | solution.py:16
  184.1 28.1 %collective-permute-start.5 = (f32[1,4096]{1,0:T(1,128)S(1)}, f32[1,4096]{1,0:T(1,128)S(1)}, u32[]{:S(2)}, u32[]{:S(2)}) collective-permute-start(f32[1,4096]{1,0:T(1,128)S(1)} %get-tuple-element.42), channel_id=1, source_target_pairs={{4,0},{8,4},{12,8},{16,12},{20,16},{24,20},{28,24},{5,1},{9,5},{13... | collective-permute-start | bytes 49160 | tf_op jit(solution)/shard_map/ppermute | solution.py:19
  205.7 10.5 %copy-start = (f32[256,4096]{1,0:T(8,128)}, f32[256,4096]{1,0:T(8,128)S(1)}, u32[]{:S(2)}) copy-start(f32[256,4096]{1,0:T(8,128)S(1)} %get-tuple-element.13) | copy-start | bytes 12582916
  205.8 9.2 %collective-permute-start.20 = (f32[1,4096]{1,0:T(1,128)S(1)}, f32[1,4096]{1,0:T(1,128)S(1)}, u32[]{:S(2)}, u32[]{:S(2)}) collective-permute-start(f32[1,4096]{1,0:T(1,128)S(1)} %get-tuple-element.51), channel_id=1, source_target_pairs={{0,4},{4,8},{8,12},{12,16},{16,20},{20,24},{24,28},{1,5},{5,9},{9,... | collective-permute-start | bytes 49160 | tf_op jit(solution)/shard_map/ppermute | solution.py:16
  210.3 6.0 collective-permute-start.21
  212.4 8.2 %collective-permute-start.6 = (f32[258,1]{1,0:T(8,128)S(1)}, f32[258,1]{1,0:T(8,128)S(1)}, u32[]{:S(2)}, u32[]{:S(2)}) collective-permute-start(f32[258,1]{1,0:T(8,128)S(1)} %get-tuple-element.27), channel_id=1, source_target_pairs={{0,1},{1,2},{2,3},{4,5},{5,6},{6,7},{8,9},{9,10},{10,11},{12,13},{... | collective-permute-start | bytes 3104 | tf_op jit(solution)/shard_map/ppermute | solution.py:16
  213.7 7.3 %collective-permute-start.7 = (f32[258,1]{1,0:T(8,128)S(1)}, f32[258,1]{1,0:T(8,128)S(1)}, u32[]{:S(2)}, u32[]{:S(2)}) collective-permute-start(f32[258,1]{1,0:T(8,128)S(1)} %get-tuple-element.26), channel_id=1, source_target_pairs={{1,0},{2,1},{3,2},{5,4},{6,5},{7,6},{9,8},{10,9},{11,10},{13,12},{... | collective-permute-start | bytes 3104 | tf_op jit(solution)/shard_map/ppermute | solution.py:19
  216.3 18.3 %copy-start.22 = (f32[1,4096]{1,0:T(1,128)}, f32[1,4096]{1,0:T(1,128)S(1)}, u32[]{:S(2)}) copy-start(f32[1,4096]{1,0:T(1,128)S(1)} %collective-permute-done.21) | copy-start | bytes 49156
  216.4 26.8 %collective-permute-start.22 = (f32[258,1]{1,0:T(8,128)S(1)}, f32[258,1]{1,0:T(8,128)S(1)}, u32[]{:S(2)}, u32[]{:S(2)}) collective-permute-start(f32[258,1]{1,0:T(8,128)S(1)} %get-tuple-element.35), channel_id=1, source_target_pairs={{0,1},{1,2},{2,3},{4,5},{5,6},{6,7},{8,9},{9,10},{10,11},{12,13},{... | collective-permute-start | bytes 3104 | tf_op jit(solution)/shard_map/ppermute | solution.py:16
  219.3 23.9 %collective-permute-start.23 = (f32[258,1]{1,0:T(8,128)S(1)}, f32[258,1]{1,0:T(8,128)}, u32[]{:S(2)}, u32[]{:S(2)}) collective-permute-start(f32[258,1]{1,0:T(8,128)S(1)} %get-tuple-element.34), channel_id=1, source_target_pairs={{1,0},{2,1},{3,2},{5,4},{6,5},{7,6},{9,8},{10,9},{11,10},{13,12},{... | collective-permute-start | bytes 3104 | tf_op jit(solution)/shard_map/ppermute | solution.py:19
  221.3 0.7 copy-start.16
  236.2 32.9 %collective-permute-start.8 = (f32[1,4096]{1,0:T(1,128)}, f32[1,4096]{1,0:T(1,128)S(1)}, u32[]{:S(2)}, u32[]{:S(2)}) collective-permute-start(f32[1,4096]{1,0:T(1,128)} %get-tuple-element.41), channel_id=1, source_target_pairs={{0,4},{4,8},{8,12},{12,16},{16,20},{20,24},{24,28},{1,5},{5,9},{9,... | collective-permute-start | bytes 49160 | tf_op jit(solution)/shard_map/ppermute | solution.py:16
  241.3 27.8 %collective-permute-start.9 = (f32[1,4096]{1,0:T(1,128)}, f32[1,4096]{1,0:T(1,128)S(1)}, u32[]{:S(2)}, u32[]{:S(2)}) collective-permute-start(f32[1,4096]{1,0:T(1,128)} %get-tuple-element.40), channel_id=1, source_target_pairs={{4,0},{8,4},{12,8},{16,12},{20,16},{24,20},{28,24},{5,1},{9,5},{13... | collective-permute-start | bytes 49160 | tf_op jit(solution)/shard_map/ppermute | solution.py:19
  261.3 14.5 %copy-start.3 = (f32[256,4096]{1,0:T(8,128)S(1)}, f32[256,4096]{1,0:T(8,128)}, u32[]{:S(2)}) copy-start(f32[256,4096]{1,0:T(8,128)} %add_add_fusion.2) | copy-start | bytes 12582916
  262.4 13.3 %collective-permute-start.24 = (f32[1,4096]{1,0:T(1,128)S(1)}, f32[1,4096]{1,0:T(1,128)S(1)}, u32[]{:S(2)}, u32[]{:S(2)}) collective-permute-start(f32[1,4096]{1,0:T(1,128)S(1)} %get-tuple-element.49), channel_id=1, source_target_pairs={{0,4},{4,8},{8,12},{12,16},{16,20},{20,24},{24,28},{1,5},{5,9},{9,... | collective-permute-start | bytes 49160 | tf_op jit(solution)/shard_map/ppermute | solution.py:16
  267.1 8.6 %collective-permute-start.25 = (f32[1,4096]{1,0:T(1,128)S(1)}, f32[1,4096]{1,0:T(1,128)S(1)}, u32[]{:S(2)}, u32[]{:S(2)}) collective-permute-start(f32[1,4096]{1,0:T(1,128)S(1)} %get-tuple-element.48), channel_id=1, source_target_pairs={{4,0},{8,4},{12,8},{16,12},{20,16},{24,20},{28,24},{5,1},{9,5},{13... | collective-permute-start | bytes 49160 | tf_op jit(solution)/shard_map/ppermute | solution.py:19
  270.1 11.7 %collective-permute-start.10 = (f32[258,1]{1,0:T(8,128)S(1)}, f32[258,1]{1,0:T(8,128)S(1)}, u32[]{:S(2)}, u32[]{:S(2)}) collective-permute-start(f32[258,1]{1,0:T(8,128)S(1)} %get-tuple-element.25), channel_id=1, source_target_pairs={{0,1},{1,2},{2,3},{4,5},{5,6},{6,7},{8,9},{9,10},{10,11},{12,13},{... | collective-permute-start | bytes 3104 | tf_op jit(solution)/shard_map/ppermute | solution.py:16
  274.4 8.1 %collective-permute-start.11 = (f32[258,1]{1,0:T(8,128)S(1)}, f32[258,1]{1,0:T(8,128)}, u32[]{:S(2)}, u32[]{:S(2)}) collective-permute-start(f32[258,1]{1,0:T(8,128)S(1)} %get-tuple-element.24), channel_id=1, source_target_pairs={{1,0},{2,1},{3,2},{5,4},{6,5},{7,6},{9,8},{10,9},{11,10},{13,12},{... | collective-permute-start | bytes 3104 | tf_op jit(solution)/shard_map/ppermute | solution.py:19
  276.3 33.9 %collective-permute-start.26 = (f32[258,1]{1,0:T(8,128)S(1)}, f32[258,1]{1,0:T(8,128)S(1)}, u32[]{:S(2)}, u32[]{:S(2)}) collective-permute-start(f32[258,1]{1,0:T(8,128)S(1)} %get-tuple-element.33), channel_id=1, source_target_pairs={{0,1},{1,2},{2,3},{4,5},{5,6},{6,7},{8,9},{9,10},{10,11},{12,13},{... | collective-permute-start | bytes 3104 | tf_op jit(solution)/shard_map/ppermute | solution.py:16
  280.3 29.9 %collective-permute-start.27 = (f32[258,1]{1,0:T(8,128)S(1)}, f32[258,1]{1,0:T(8,128)}, u32[]{:S(2)}, u32[]{:S(2)}) collective-permute-start(f32[258,1]{1,0:T(8,128)S(1)} %get-tuple-element.32), channel_id=1, source_target_pairs={{1,0},{2,1},{3,2},{5,4},{6,5},{7,6},{9,8},{10,9},{11,10},{13,12},{... | collective-permute-start | bytes 3104 | tf_op jit(solution)/shard_map/ppermute | solution.py:19
  302.9 33.3 %collective-permute-start.12 = (f32[1,4096]{1,0:T(1,128)}, f32[1,4096]{1,0:T(1,128)S(1)}, u32[]{:S(2)}, u32[]{:S(2)}) collective-permute-start(f32[1,4096]{1,0:T(1,128)} %get-tuple-element.38), channel_id=1, source_target_pairs={{0,4},{4,8},{8,12},{12,16},{16,20},{20,24},{24,28},{1,5},{5,9},{9,... | collective-permute-start | bytes 49160 | tf_op jit(solution)/shard_map/ppermute | solution.py:16
  308.3 28.0 %collective-permute-start.13 = (f32[1,4096]{1,0:T(1,128)S(1)}, f32[1,4096]{1,0:T(1,128)S(1)}, u32[]{:S(2)}, u32[]{:S(2)}) collective-permute-start(f32[1,4096]{1,0:T(1,128)S(1)} %get-tuple-element.39), channel_id=1, source_target_pairs={{4,0},{8,4},{12,8},{16,12},{20,16},{24,20},{28,24},{5,1},{9,5},{13... | collective-permute-start | bytes 49160 | tf_op jit(solution)/shard_map/ppermute | solution.py:19
  329.3 13.7 %collective-permute-start.28 = (f32[1,4096]{1,0:T(1,128)S(1)}, f32[1,4096]{1,0:T(1,128)S(1)}, u32[]{:S(2)}, u32[]{:S(2)}) collective-permute-start(f32[1,4096]{1,0:T(1,128)S(1)} %get-tuple-element.46), channel_id=1, source_target_pairs={{0,4},{4,8},{8,12},{12,16},{16,20},{20,24},{24,28},{1,5},{5,9},{9,... | collective-permute-start | bytes 49160 | tf_op jit(solution)/shard_map/ppermute | solution.py:16
  333.9 17.4 %copy-start.2 = (f32[256,4096]{1,0:T(8,128)S(1)}, f32[256,4096]{1,0:T(8,128)}, u32[]{:S(2)}) copy-start(f32[256,4096]{1,0:T(8,128)} %add_add_fusion.6) | copy-start | bytes 12582916
  333.9 17.4 %copy-start.6 = (bf16[1,4,64,4096]{3,2,1,0:T(8,128)(2,1)S(1)}, bf16[1,4,64,4096]{3,2,1,0:T(8,128)(2,1)}, u32[]{:S(2)}) copy-start(bf16[1,4,64,4096]{3,2,1,0:T(8,128)(2,1)} %copy-done.5) | copy-start | bytes 6291460
  333.9 17.4 %copy-start.9 = (pred[256,4096]{1,0:T(8,128)(4,1)S(1)}, pred[256,4096]{1,0:T(8,128)(4,1)}, u32[]{:S(2)}) copy-start(pred[256,4096]{1,0:T(8,128)(4,1)} %get-tuple-element.9) | copy-start | bytes 3145732
  333.9 17.4 %copy-start.10 = (pred[256,4096]{1,0:T(8,128)(4,1)S(1)}, pred[256,4096]{1,0:T(8,128)(4,1)}, u32[]{:S(2)}) copy-start(pred[256,4096]{1,0:T(8,128)(4,1)} %get-tuple-element.10) | copy-start | bytes 3145732
  333.9 17.4 %copy-start.26 = (pred[256]{0:T(512)(128)(4,1)S(1)}, pred[256]{0:T(512)(128)(4,1)}, u32[]{:S(2)}) copy-start(pred[256]{0:T(512)(128)(4,1)} %copy-done.25) | copy-start | bytes 772
  333.9 9.1 %collective-permute-start.29 = (f32[1,4096]{1,0:T(1,128)S(1)}, f32[1,4096]{1,0:T(1,128)S(1)}, u32[]{:S(2)}, u32[]{:S(2)}) collective-permute-start(f32[1,4096]{1,0:T(1,128)S(1)} %get-tuple-element.47), channel_id=1, source_target_pairs={{4,0},{8,4},{12,8},{16,12},{20,16},{24,20},{28,24},{5,1},{9,5},{13... | collective-permute-start | bytes 49160 | tf_op jit(solution)/shard_map/ppermute | solution.py:19
  336.3 6.8 %copy-start.19 = (f32[1,4096]{1,0:T(1,128)}, f32[1,4096]{1,0:T(1,128)S(1)}, u32[]{:S(2)}) copy-start(f32[1,4096]{1,0:T(1,128)S(1)} %collective-permute-done.13) | copy-start | bytes 49156
  337.4 13.9 %collective-permute-start.14 = (f32[258,1]{1,0:T(8,128)S(1)}, f32[258,1]{1,0:T(8,128)S(1)}, u32[]{:S(2)}, u32[]{:S(2)}) collective-permute-start(f32[258,1]{1,0:T(8,128)S(1)} %get-tuple-element.22), channel_id=1, source_target_pairs={{0,1},{1,2},{2,3},{4,5},{5,6},{6,7},{8,9},{9,10},{10,11},{12,13},{... | collective-permute-start | bytes 3104 | tf_op jit(solution)/shard_map/ppermute | solution.py:16
  341.7 9.6 %collective-permute-start.15 = (f32[258,1]{1,0:T(8,128)S(1)}, f32[258,1]{1,0:T(8,128)S(1)}, u32[]{:S(2)}, u32[]{:S(2)}) collective-permute-start(f32[258,1]{1,0:T(8,128)S(1)} %get-tuple-element.23), channel_id=1, source_target_pairs={{1,0},{2,1},{3,2},{5,4},{6,5},{7,6},{9,8},{10,9},{11,10},{13,12},{... | collective-permute-start | bytes 3104 | tf_op jit(solution)/shard_map/ppermute | solution.py:19
  343.0 29.3 %copy-start.17 = (f32[1,4096]{1,0:T(1,128)}, f32[1,4096]{1,0:T(1,128)S(1)}, u32[]{:S(2)}) copy-start(f32[1,4096]{1,0:T(1,128)S(1)} %collective-permute-done.28) | copy-start | bytes 49156
  343.1 29.2 %copy-start.21 = (f32[1,4096]{1,0:T(1,128)}, f32[1,4096]{1,0:T(1,128)S(1)}, u32[]{:S(2)}) copy-start(f32[1,4096]{1,0:T(1,128)S(1)} %collective-permute-done.29) | copy-start | bytes 49156
  343.1 8.3 %copy-start.20 = (f32[1,4096]{1,0:T(1,128)S(1)}, f32[1,4096]{1,0:T(1,128)}, u32[]{:S(2)}) copy-start(f32[1,4096]{1,0:T(1,128)} %copy-done.19) | copy-start | bytes 49156
  344.8 36.2 %collective-permute-start.30 = (f32[258,1]{1,0:T(8,128)}, f32[258,1]{1,0:T(8,128)S(1)}, u32[]{:S(2)}, u32[]{:S(2)}) collective-permute-start(f32[258,1]{1,0:T(8,128)} %get-tuple-element.30), channel_id=1, source_target_pairs={{0,1},{1,2},{2,3},{4,5},{5,6},{6,7},{8,9},{9,10},{10,11},{12,13},{... | collective-permute-start | bytes 3104 | tf_op jit(solution)/shard_map/ppermute | solution.py:16
  349.6 31.4 %collective-permute-start.31 = (f32[258,1]{1,0:T(8,128)S(1)}, f32[258,1]{1,0:T(8,128)S(1)}, u32[]{:S(2)}, u32[]{:S(2)}) collective-permute-start(f32[258,1]{1,0:T(8,128)S(1)} %get-tuple-element.31), channel_id=1, source_target_pairs={{1,0},{2,1},{3,2},{5,4},{6,5},{7,6},{9,8},{10,9},{11,10},{13,12},{... | collective-permute-start | bytes 3104 | tf_op jit(solution)/shard_map/ppermute | solution.py:19
  372.3 8.7 %copy-start.1 = (f32[256,4096]{1,0:T(8,128)S(1)}, f32[256,4096]{1,0:T(8,128)}, u32[]{:S(2)}) copy-start(f32[256,4096]{1,0:T(8,128)} %copy-done) | copy-start | bytes 12582916
  372.3 8.7 %copy-start.4 = (bf16[1,4,64,4096]{3,2,1,0:T(8,128)(2,1)S(1)}, bf16[1,4,64,4096]{3,2,1,0:T(8,128)(2,1)}, u32[]{:S(2)}) copy-start(bf16[1,4,64,4096]{3,2,1,0:T(8,128)(2,1)} %get-tuple-element.45) | copy-start | bytes 6291460
  372.3 8.7 %copy-start.18 = (f32[1,4096]{1,0:T(1,128)S(1)}, f32[1,4096]{1,0:T(1,128)}, u32[]{:S(2)}) copy-start(f32[1,4096]{1,0:T(1,128)} %copy-done.17) | copy-start | bytes 49156
  400.6 4.7 copy-start.11
  414.4 189.9 %all-to-all-start.1 = ((f32[2,256,4096]{2,0,1:T(2,128)}), f32[2,256,4096]{2,0,1:T(2,128)}, u32[]{:S(2)}, u32[]{:S(2)}) async-start(f32[2,256,4096]{2,0,1:T(2,128)} %pad_maximum_fusion), calls=%async_computation.1 | async-start | bytes 16777216 | tf_op jit(solution)/shard_map/all_to_all | solution.py:76
  (4 other events, 2.6 us)
where the time goes:
time: 638 us; the launch traced here: 628 us
  waiting for transfers between devices  242 us (38%)
  other arithmetic  169 us (26%)
  local copies, waits for them, and re-layouts  109 us (17%)
  starting transfers between devices  106 us (17%)
    all_to_all x1, waiting for transfers between devices, body(): lax.all_to_all(jnp.stack(phases), 'cols', split_axis=1, concat_axis=2, ti...  175 us
    add x6, other arithmetic, advance(): middle - jnp.abs(wind_x) * (middle - upwind_x)  107 us
    ppermute x16, starting transfers between devices, extended(): lax.ppermute(lax.slice_in_dim(block, block.shape[dim] - width, None, axis...  67.2 us
    all_to_all x1, waiting for transfers between devices, body(): lax.all_to_all(irradiance_layers, 'cols', split_axis=2, concat_axis=1, ti...  64.7 us
    unnamed x71, local copies, waits for them, and re-layouts  39.5 us
    another operation x2, other arithmetic, body(): jnp.stack(phases)  30.1 us
    ppermute x16, starting transfers between devices, extended(): lax.ppermute(lax.slice_in_dim(block, 0, width, axis=dim), axis, backward)  26.7 us
    all_to_all x2, local copies, waits for them, and re-layouts, body(): lax.all_to_all(jnp.stack(phases), 'cols', split_axis=1, concat_axis=2, ti...  23 us
  transfers between devices with their start and end apart: 34, of which 4 were waited for; matrix products, arithmetic and copies ran while one was open for 31% of the time, Pallas kernels for 0%

commit v1 on v0

--- a/solution.py
+++ b/solution.py
@@ -73,7 +73,13 @@
             phase_sum = phase_sum + heat_transport_advance / SUBSTEPS
         phases.append(phase_sum)
         finals.append(heat_transport_advance)
-    phase_slabs = lax.all_to_all(jnp.stack(phases), "cols", split_axis=1, concat_axis=2, tiled=True)
+    extend_wall = lambda inp, axis_id: jnp.concatenate(
+        lax.all_to_all(
+            jnp.stack(jnp.split(inp, lax.axis_size(axis_id), axis=1), axis=0), axis_id, 0, 0
+        ),
+        axis=2,
+    )
+    phase_slabs = extend_wall(jnp.stack(phases), "cols")
     return (phase_slabs, jnp.stack(finals))
 
 

time: 638 us -> 607 us (0.951)
  local copies, waits for them, and re-layouts: 109 us -> 80.5 us
    all_to_all x2 -> x0, local copies, waits for them, and re-layouts: 23 us -> none  [body(): lax.all_to_all(jnp.stack(phases), 'cols', split_axis=1, concat_axis=2, ti...]
    add x1 -> x0, other arithmetic: 19.5 us -> none  [body(): phase_sum = phase_sum + heat_transport_advance / SUBSTEPS]
    another operation x2 -> x4, other arithmetic: 30.1 us -> 47.9 us  [the longest x2 41.6 us: body(): phase_slabs = extend_wall(jnp.stack(phases), 'cols')]
    another operation x2 -> x0, local copies, waits for them, and re-layouts: 13.3 us -> none  [body(): jnp.stack(phases)]
    reshape x0 -> x1, local copies, waits for them, and re-layouts: none -> 7.77 us  [body(): jnp.concatenate(lax.all_to_all(jnp.stack(jnp.split(inp, lax.axis_size(axi...]
    unnamed x71 -> x57, local copies, waits for them, and re-layouts: 39.5 us -> 39.3 us
where the time goes in v1:
time: 607 us; the launch traced here: 596 us
  waiting for transfers between devices  242 us (40%)
  other arithmetic  167 us (28%)
  starting transfers between devices  105 us (17%)
  local copies, waits for them, and re-layouts  80.5 us (13%)
    all_to_all x1, waiting for transfers between devices, body(): lax.all_to_all(jnp.stack(jnp.split(inp, lax.axis_size(axis_id), axis=1),...  176 us
    add x6, other arithmetic, advance(): middle - jnp.abs(wind_x) * (middle - upwind_x)  107 us
    ppermute x16, starting transfers between devices, extended(): lax.ppermute(lax.slice_in_dim(block, block.shape[dim] - width, None, axis...  67.7 us
    all_to_all x1, waiting for transfers between devices, body(): lax.all_to_all(irradiance_layers, 'cols', split_axis=2, concat_axis=1, ti...  64.6 us
    another operation x2, other arithmetic, body(): phase_slabs = extend_wall(jnp.stack(phases), 'cols')  41.6 us
    unnamed x57, local copies, waits for them, and re-layouts  39.3 us
    ppermute x16, starting transfers between devices, extended(): lax.ppermute(lax.slice_in_dim(block, 0, width, axis=dim), axis, backward)  26.5 us
    all_to_all x1, local copies, waits for them, and re-layouts, body(): lax.all_to_all(irradiance_layers, 'cols', split_axis=2, concat_axis=1, ti...  18.6 us
  transfers between devices with their start and end apart: 34, of which 4 were waited for; matrix products, arithmetic and copies ran while one was open for 31% of the time, Pallas kernels for 0%

profile of v1, /device:TPU:3, one launch (start us, length us, event | category | flops | bytes accessed | tf_op | source)
XLA Modules:
  0.0 596.1 jit_solution(12879038088027218814)
XLA Ops:
  0.6 17.8 %copy.18 = bf16[2,64,16384]{1,0,2:T(2,128)(2,1)} copy(bf16[2,64,16384]{2,1,0:T(8,128)(2,1)} %param.7) | data formatting | bytes 8388608 | tf_op args[0]
  18.4 9.6 %reshape.52 = bf16[4,2,262144]{2,1,0:T(2,128)(2,1)} reshape(bf16[16384,2,64]{2,1,0:T(2,128)(2,1)} %bitcast.152) | data formatting | bytes 8388608
  27.9 5.0 all-to-all-start
  33.0 1.1 slice_bitcast_fusion.4
  34.1 3.7 collective-permute-start.16
  37.8 1.9 collective-permute-start.17
  39.7 4.5 collective-permute-start
  44.3 1.9 collective-permute-start.1
  46.3 4.0 slice_bitcast_fusion.1
  50.5 3.6 collective-permute-start.18
  54.2 1.3 collective-permute-start.19
  55.6 4.0 collective-permute-start.2
  59.6 1.3 collective-permute-start.3
  60.9 64.6 %all-to-all-done = bf16[4,2,262144]{2,1,0:T(2,128)(2,1)} async-done(((bf16[4,2,262144]{2,1,0:T(2,128)(2,1)}), bf16[4,2,262144]{2,1,0:T(2,128)(2,1)}, u32[]{:S(2)}, u32[]{:S(2)}) %all-to-all-start) | async-done | bytes 4194336 | tf_op jit(solution)/shard_map/all_to_all | solution.py:52
  125.6 9.3 %reshape.53 = bf16[16384,2,64]{2,1,0:T(2,128)(2,1)} reshape(bf16[4,2,262144]{2,1,0:T(2,128)(2,1)} %all-to-all-done) | data formatting | bytes 8388608
  134.9 18.6 %copy.20 = bf16[2,64,4,4096]{3,1,2,0:T(8,128)(2,1)} copy(bf16[2,64,4,4096]{1,0,3,2:T(2,128)(2,1)} %bitcast.151) | data formatting | bytes 8388608 | tf_op jit(solution)/shard_map/all_to_all | solution.py:52
  153.5 4.2 fusion.22
  158.3 20.2 %add_add_fusion.3 = (f32[256,4096]{1,0:T(8,128)S(1)}, pred[256,4096]{1,0:T(8,128)(4,1)}, pred[256,4096]{1,0:T(8,128)(4,1)}) fusion(f32[256,4096]{1,0:T(8,128)} %copy-done.7, f32[1,4096]{1,0:T(1,128)S(1)} %collective-permute-done.16, f32[1,4096]{1,0:T(1,128)S(1)} %collective-permute-done.17, f32[258,1]{1,0:T(8,128)} %copy-done.10, f32[258,1]{1,0:T(8,128)} %copy-done.11, ...), kind=kLoop, calls=%fused_computation.82 | loop fusion | flops 36700160 | bytes 25205008 | tf_op jit(solution)/shard_map/add | solution.py:34
  178.5 5.7 collective-permute-start.20
  184.2 1.9 collective-permute-start.21
  186.2 19.6 %add_add_fusion.7 = (f32[256,4096]{1,0:T(8,128)S(1)}, pred[256,4096]{1,0:T(8,128)(4,1)}, pred[256,4096]{1,0:T(8,128)(4,1)}) fusion(f32[256,4096]{1,0:T(8,128)} %copy-done.6, f32[1,4096]{1,0:T(1,128)S(1)} %collective-permute-done, f32[1,4096]{1,0:T(1,128)S(1)} %collective-permute-done.1, f32[258,1]{1,0:T(8,128)S(1)} %collective-permute-done.2, ...), kind=kLoop, calls=%fused_computation.88 | loop fusion | flops 36700160 | bytes 25205008 | tf_op jit(solution)/shard_map/add | solution.py:34
  205.8 4.5 collective-permute-start.4
  210.4 1.9 collective-permute-start.5
  212.4 1.3 collective-permute-start.22
  213.7 1.3 collective-permute-start.23
  215.1 1.3 collective-permute-done.5
  216.4 3.2 collective-permute-start.6
  219.7 1.3 collective-permute-start.7
  222.3 12.5 %add_add_fusion.2 = f32[256,4096]{1,0:T(8,128)} fusion(f32[256,4096]{1,0:T(8,128)S(1)} %get-tuple-element.13, pred[256,4096]{1,0:T(8,128)(4,1)} %get-tuple-element.15, f32[1,4096]{1,0:T(1,128)S(1)} %collective-permute-done.20, f32[1,4096]{1,0:T(1,128)S(1)} %collective-permute-done.21, pred[256,4096]{1,0:T(8,128)(4,1)} %get-tuple-element.14, ...), kind=kLoop, calls=%fused_computation.81 | loop fusion | flops 34603008 | bytes 25205008 | tf_op jit(solution)/shard_map/add | solution.py:34
  234.8 1.6 fusion.24
  236.4 5.1 collective-permute-start.24
  241.5 1.9 collective-permute-start.25
  243.4 18.0 %add_add_fusion.6 = f32[256,4096]{1,0:T(8,128)} fusion(f32[256,4096]{1,0:T(8,128)} %copy-done, pred[256,4096]{1,0:T(8,128)(4,1)} %get-tuple-element.10, f32[1,4096]{1,0:T(1,128)S(1)} %collective-permute-done.4, f32[1,4096]{1,0:T(1,128)} %copy-done.15, pred[256,4096]{1,0:T(8,128)(4,1)} %get-tuple-element.9, f32[258,1]{1,0:T(8,128)S(1)} %collective-permute-done.6, ...), kind=kLoop, calls=%fused_computation.87 | loop fusion | flops 34603008 | bytes 25205008 | tf_op jit(solution)/shard_map/add | solution.py:34
  261.5 1.1 fusion.20
  262.6 4.7 collective-permute-start.8
  267.3 1.9 collective-permute-start.9
  269.3 1.1 pad_maximum_fusion.70
  270.4 4.3 collective-permute-start.26
  274.6 1.3 collective-permute-start.27
  276.1 4.0 collective-permute-start.10
  280.1 1.5 collective-permute-start.11
  281.6 0.7 copy-done.13
  282.3 18.9 %add_add_fusion.1 = f32[256,4096]{1,0:T(8,128)} fusion(f32[256,4096]{1,0:T(8,128)} %add_add_fusion.2, pred[256,4096]{1,0:T(8,128)(4,1)} %get-tuple-element.15, f32[1,4096]{1,0:T(1,128)S(1)} %collective-permute-done.24, f32[1,4096]{1,0:T(1,128)S(1)} %collective-permute-done.25, pred[256,4096]{1,0:T(8,128)(4,1)} %get-tuple-element.14, f32[258,1]{1,0:T(8,128)} %copy-done.13, ...), kind=kLoop, calls=%fused_computation.80 | loop fusion | flops 34603008 | bytes 25205008 | tf_op jit(solution)/shard_map/add | solution.py:34
  301.2 1.6 fusion.23
  302.8 5.4 collective-permute-start.28
  308.2 1.9 collective-permute-start.29
  310.1 18.1 %add_add_fusion.5 = f32[256,4096]{1,0:T(8,128)} fusion(f32[256,4096]{1,0:T(8,128)} %add_add_fusion.6, pred[256,4096]{1,0:T(8,128)(4,1)} %get-tuple-element.10, f32[1,4096]{1,0:T(1,128)S(1)} %collective-permute-done.8, f32[1,4096]{1,0:T(1,128)} %copy-done.16, pred[256,4096]{1,0:T(8,128)(4,1)} %get-tuple-element.9, f32[258,1]{1,0:T(8,128)S(1)} %collective-permute-done.10, ...), kind=kLoop, calls=%fused_computation.86 | loop fusion | flops 34603008 | bytes 25205008 | tf_op jit(solution)/shard_map/add | solution.py:34
  328.3 1.1 fusion.19
  329.4 4.7 collective-permute-start.12
  334.1 2.1 collective-permute-start.13
  336.2 1.1 pad_maximum_fusion.69
  337.3 4.3 collective-permute-start.30
  341.6 1.3 collective-permute-start.31
  342.9 0.8 pad_maximum_fusion.81
  343.7 4.8 collective-permute-start.14
  348.5 1.8 collective-permute-start.15
  350.3 20.4 %multiply_bitcast_fusion = (f32[1,256,4096]{2,1,0:T(8,128)}, f32[256,4096]{1,0:T(8,128)}) fusion(f32[256,4096]{1,0:T(8,128)} %add_add_fusion.1, f32[256,4096]{1,0:T(8,128)S(1)} %get-tuple-element.13, f32[256,4096]{1,0:T(8,128)} %add_add_fusion.2, bf16[1,4,64,4096]{3,2,1,0:T(8,128)(2,1)} %copy-done.4, f32[2,256,4096]{2,1,0:T(8,128)} %param.11, ...), kind=kLoop, calls=%fused_computation.78 | loop fusion | flops 38797312 | bytes 37787920 | tf_op jit(solution)/shard_map/stack | solution.py:82
  370.8 21.2 %multiply_bitcast_fusion.1 = (f32[1,256,4096]{2,1,0:T(8,128)}, f32[256,4096]{1,0:T(8,128)}) fusion(f32[256,4096]{1,0:T(8,128)} %add_add_fusion.5, f32[256,4096]{1,0:T(8,128)S(1)} %copy-done.1, f32[256,4096]{1,0:T(8,128)} %add_add_fusion.6, bf16[1,4,64,4096]{3,2,1,0:T(8,128)(2,1)S(1)} %copy-done.3, f32[2,256,4096]{2,1,0:T(8,128)S(1)} %bitcast.148, ...), kind=kLoop, calls=%fused_computation.84 | loop fusion | flops 38797312 | bytes 37787920 | tf_op jit(solution)/shard_map/stack | solution.py:82
  391.9 2.6 fusion.11
  394.6 3.7 pad_maximum_fusion
  398.3 5.9 all-to-all-start.1
  404.2 7.9 %pad_maximum_fusion.1 = f32[2,256,4096]{2,1,0:T(8,128)} fusion(f32[1,256,4096]{2,1,0:T(8,128)} %bitcast.154, f32[1,256,4096]{2,1,0:T(8,128)} %bitcast.155), kind=kLoop, calls=%fused_computation.7 | loop fusion | flops 2097152 | bytes 16777216 | tf_op jit(solution)/shard_map/stack | solution.py:83
  412.0 176.1 %all-to-all-done.1 = f32[4,2,64,4096]{3,2,1,0:T(8,128)} async-done(((f32[4,2,64,4096]{3,2,1,0:T(8,128)}), f32[4,2,64,4096]{3,2,1,0:T(8,128)}, u32[]{:S(2)}, u32[]{:S(2)}) %all-to-all-start.1) | async-done | bytes 8388640 | tf_op jit(solution)/shard_map/all_to_all | solution.py:77
  588.1 7.8 %copy.24 = f32[4,2,8,8,4096]{4,3,0,2,1:T(8,128)} copy(f32[4,2,8,8,4096]{4,3,2,1,0:T(8,128)} %bitcast.27) | data formatting | bytes 16777216 | tf_op jit(solution)/shard_map/reshape | solution.py:76
  (97 shorter events, 2.9 us)
Async XLA Ops:
  27.9 18.3 %copy-start.17 = (s32[2,4096]{1,0:T(2,128)S(1)}, s32[2,4096]{1,0:T(2,128)}, u32[]{:S(2)}) copy-start(s32[2,4096]{1,0:T(2,128)} %param.13) | copy-start | bytes 98308
  27.9 97.6 %all-to-all-start = ((bf16[4,2,262144]{2,1,0:T(2,128)(2,1)}), bf16[4,2,262144]{2,1,0:T(2,128)(2,1)}, u32[]{:S(2)}, u32[]{:S(2)}) async-start(bf16[4,2,262144]{2,1,0:T(2,128)(2,1)} %reshape.52), calls=%async_computation | async-start | bytes 8388608 | tf_op jit(solution)/shard_map/all_to_all | solution.py:52
  34.1 16.3 %collective-permute-start.16 = (f32[1,4096]{1,0:T(1,128)S(1)}, f32[1,4096]{1,0:T(1,128)S(1)}, u32[]{:S(2)}, u32[]{:S(2)}) collective-permute-start(f32[1,4096]{1,0:T(1,128)S(1)} %get-tuple-element.23), channel_id=1, source_target_pairs={{0,4},{4,8},{8,12},{12,16},{16,20},{20,24},{24,28},{1,5},{5,9},{9,... | collective-permute-start | bytes 49160 | tf_op jit(solution)/shard_map/ppermute | solution.py:16
  37.8 12.6 %collective-permute-start.17 = (f32[1,4096]{1,0:T(1,128)S(1)}, f32[1,4096]{1,0:T(1,128)S(1)}, u32[]{:S(2)}, u32[]{:S(2)}) collective-permute-start(f32[1,4096]{1,0:T(1,128)S(1)} %get-tuple-element.22), channel_id=1, source_target_pairs={{4,0},{8,4},{12,8},{16,12},{20,16},{24,20},{28,24},{5,1},{9,5},{13... | collective-permute-start | bytes 49160 | tf_op jit(solution)/shard_map/ppermute | solution.py:19
  39.7 15.8 %collective-permute-start = (f32[1,4096]{1,0:T(1,128)S(1)}, f32[1,4096]{1,0:T(1,128)S(1)}, u32[]{:S(2)}, u32[]{:S(2)}) collective-permute-start(f32[1,4096]{1,0:T(1,128)S(1)} %get-tuple-element.21), channel_id=1, source_target_pairs={{0,4},{4,8},{8,12},{12,16},{16,20},{20,24},{24,28},{1,5},{5,9},{9,... | collective-permute-start | bytes 49160 | tf_op jit(solution)/shard_map/ppermute | solution.py:16
  44.3 11.2 %collective-permute-start.1 = (f32[1,4096]{1,0:T(1,128)S(1)}, f32[1,4096]{1,0:T(1,128)S(1)}, u32[]{:S(2)}, u32[]{:S(2)}) collective-permute-start(f32[1,4096]{1,0:T(1,128)S(1)} %get-tuple-element.20), channel_id=1, source_target_pairs={{4,0},{8,4},{12,8},{16,12},{20,16},{24,20},{28,24},{5,1},{9,5},{13... | collective-permute-start | bytes 49160 | tf_op jit(solution)/shard_map/ppermute | solution.py:19
  46.3 4.0 copy-start.18
  50.4 5.3 copy-start.6
  50.4 5.3 copy-start.7
  50.5 107.1 %collective-permute-start.18 = (f32[258,1]{1,0:T(8,128)S(1)}, f32[258,1]{1,0:T(8,128)S(1)}, u32[]{:S(2)}, u32[]{:S(2)}) collective-permute-start(f32[258,1]{1,0:T(8,128)S(1)} %get-tuple-element.41), channel_id=1, source_target_pairs={{0,1},{1,2},{2,3},{4,5},{5,6},{6,7},{8,9},{9,10},{10,11},{12,13},{... | collective-permute-start | bytes 3104 | tf_op jit(solution)/shard_map/ppermute | solution.py:16
  54.2 103.4 %collective-permute-start.19 = (f32[258,1]{1,0:T(8,128)S(1)}, f32[258,1]{1,0:T(8,128)S(1)}, u32[]{:S(2)}, u32[]{:S(2)}) collective-permute-start(f32[258,1]{1,0:T(8,128)S(1)} %get-tuple-element.40), channel_id=1, source_target_pairs={{1,0},{2,1},{3,2},{5,4},{6,5},{7,6},{9,8},{10,9},{11,10},{13,12},{... | collective-permute-start | bytes 3104 | tf_op jit(solution)/shard_map/ppermute | solution.py:19
  55.6 130.5 %collective-permute-start.2 = (f32[258,1]{1,0:T(8,128)S(1)}, f32[258,1]{1,0:T(8,128)S(1)}, u32[]{:S(2)}, u32[]{:S(2)}) collective-permute-start(f32[258,1]{1,0:T(8,128)S(1)} %get-tuple-element.33), channel_id=1, source_target_pairs={{0,1},{1,2},{2,3},{4,5},{5,6},{6,7},{8,9},{9,10},{10,11},{12,13},{... | collective-permute-start | bytes 3104 | tf_op jit(solution)/shard_map/ppermute | solution.py:16
  59.6 126.5 %collective-permute-start.3 = (f32[258,1]{1,0:T(8,128)S(1)}, f32[258,1]{1,0:T(8,128)}, u32[]{:S(2)}, u32[]{:S(2)}) collective-permute-start(f32[258,1]{1,0:T(8,128)S(1)} %get-tuple-element.32), channel_id=1, source_target_pairs={{1,0},{2,1},{3,2},{5,4},{6,5},{7,6},{9,8},{10,9},{11,10},{13,12},{... | collective-permute-start | bytes 3104 | tf_op jit(solution)/shard_map/ppermute | solution.py:19
  153.4 32.7 %slice-start = ((s8[8388608]{0:T(1024)(128)(4,1)}), s8[4194304]{0:T(1024)(128)(4,1)S(1)}, s32[]{:S(2)}) async-start(s8[8388608]{0:T(1024)(128)(4,1)} %bitcast.143), calls=%async_computation.2 | async-start | bytes 8388608
  153.4 32.7 %slice-start.2 = ((s8[8388608]{0:T(1024)(128)(4,1)}), s8[4194304]{0:T(1024)(128)(4,1)S(1)}, s32[]{:S(2)}) async-start(s8[8388608]{0:T(1024)(128)(4,1)} %bitcast.145), calls=%async_computation.4 | async-start | bytes 8388608
  153.5 32.7 %slice-start.6 = ((s8[8388608]{0:T(1024)(128)(4,1)}), s8[4194304]{0:T(1024)(128)(4,1)S(1)}, s32[]{:S(2)}) async-start(s8[8388608]{0:T(1024)(128)(4,1)} %bitcast.149), calls=%async_computation.8 | async-start | bytes 8388608
  157.6 20.9 %copy-start.4 = (bf16[1,4,64,4096]{3,2,1,0:T(8,128)(2,1)}, bf16[1,4,64,4096]{3,2,1,0:T(8,128)(2,1)S(1)}, u32[]{:S(2)}) copy-start(bf16[1,4,64,4096]{3,2,1,0:T(8,128)(2,1)S(1)} %get-tuple-element.49) | copy-start | bytes 6291460
  157.6 0.7 copy-start.10
  157.6 0.7 copy-start.11
  158.3 27.9 %slice-start.1 = ((s8[8388608]{0:T(1024)(128)(4,1)}), s8[4194304]{0:T(1024)(128)(4,1)S(1)}, s32[]{:S(2)}) async-start(s8[8388608]{0:T(1024)(128)(4,1)} %bitcast.143), calls=%async_computation.3 | async-start | bytes 8388608
  158.3 27.9 %slice-start.3 = ((s8[8388608]{0:T(1024)(128)(4,1)}), s8[4194304]{0:T(1024)(128)(4,1)S(1)}, s32[]{:S(2)}) async-start(s8[8388608]{0:T(1024)(128)(4,1)} %bitcast.145), calls=%async_computation.5 | async-start | bytes 8388608
  158.3 27.9 %slice-start.7 = ((s8[8388608]{0:T(1024)(128)(4,1)}), s8[4194304]{0:T(1024)(128)(4,1)S(1)}, s32[]{:S(2)}) async-start(s8[8388608]{0:T(1024)(128)(4,1)} %bitcast.149), calls=%async_computation.9 | async-start | bytes 8388608
  178.5 33.8 %collective-permute-start.20 = (f32[1,4096]{1,0:T(1,128)S(1)}, f32[1,4096]{1,0:T(1,128)S(1)}, u32[]{:S(2)}, u32[]{:S(2)}) collective-permute-start(f32[1,4096]{1,0:T(1,128)S(1)} %get-tuple-element.55), channel_id=1, source_target_pairs={{0,4},{4,8},{8,12},{12,16},{16,20},{20,24},{24,28},{1,5},{5,9},{9,... | collective-permute-start | bytes 49160 | tf_op jit(solution)/shard_map/ppermute | solution.py:16
  184.2 28.1 %collective-permute-start.21 = (f32[1,4096]{1,0:T(1,128)S(1)}, f32[1,4096]{1,0:T(1,128)S(1)}, u32[]{:S(2)}, u32[]{:S(2)}) collective-permute-start(f32[1,4096]{1,0:T(1,128)S(1)} %get-tuple-element.54), channel_id=1, source_target_pairs={{4,0},{8,4},{12,8},{16,12},{20,16},{24,20},{28,24},{5,1},{9,5},{13... | collective-permute-start | bytes 49160 | tf_op jit(solution)/shard_map/ppermute | solution.py:19
  205.8 10.5 %copy-start = (f32[256,4096]{1,0:T(8,128)}, f32[256,4096]{1,0:T(8,128)S(1)}, u32[]{:S(2)}) copy-start(f32[256,4096]{1,0:T(8,128)S(1)} %get-tuple-element.8) | copy-start | bytes 12582916
  205.8 9.2 %collective-permute-start.4 = (f32[1,4096]{1,0:T(1,128)S(1)}, f32[1,4096]{1,0:T(1,128)S(1)}, u32[]{:S(2)}, u32[]{:S(2)}) collective-permute-start(f32[1,4096]{1,0:T(1,128)S(1)} %get-tuple-element.47), channel_id=1, source_target_pairs={{0,4},{4,8},{8,12},{12,16},{16,20},{20,24},{24,28},{1,5},{5,9},{9,... | collective-permute-start | bytes 49160 | tf_op jit(solution)/shard_map/ppermute | solution.py:16
  210.4 6.0 collective-permute-start.5
  212.4 8.5 %collective-permute-start.22 = (f32[258,1]{1,0:T(8,128)S(1)}, f32[258,1]{1,0:T(8,128)S(1)}, u32[]{:S(2)}, u32[]{:S(2)}) collective-permute-start(f32[258,1]{1,0:T(8,128)S(1)} %get-tuple-element.39), channel_id=1, source_target_pairs={{0,1},{1,2},{2,3},{4,5},{5,6},{6,7},{8,9},{9,10},{10,11},{12,13},{... | collective-permute-start | bytes 3104 | tf_op jit(solution)/shard_map/ppermute | solution.py:16
  213.7 7.3 %collective-permute-start.23 = (f32[258,1]{1,0:T(8,128)S(1)}, f32[258,1]{1,0:T(8,128)S(1)}, u32[]{:S(2)}, u32[]{:S(2)}) collective-permute-start(f32[258,1]{1,0:T(8,128)S(1)} %get-tuple-element.38), channel_id=1, source_target_pairs={{1,0},{2,1},{3,2},{5,4},{6,5},{7,6},{9,8},{10,9},{11,10},{13,12},{... | collective-permute-start | bytes 3104 | tf_op jit(solution)/shard_map/ppermute | solution.py:19
  216.3 18.4 %copy-start.15 = (f32[1,4096]{1,0:T(1,128)}, f32[1,4096]{1,0:T(1,128)S(1)}, u32[]{:S(2)}) copy-start(f32[1,4096]{1,0:T(1,128)S(1)} %collective-permute-done.5) | copy-start | bytes 49156
  216.4 27.0 %collective-permute-start.6 = (f32[258,1]{1,0:T(8,128)S(1)}, f32[258,1]{1,0:T(8,128)S(1)}, u32[]{:S(2)}, u32[]{:S(2)}) collective-permute-start(f32[258,1]{1,0:T(8,128)S(1)} %get-tuple-element.31), channel_id=1, source_target_pairs={{0,1},{1,2},{2,3},{4,5},{5,6},{6,7},{8,9},{9,10},{10,11},{12,13},{... | collective-permute-start | bytes 3104 | tf_op jit(solution)/shard_map/ppermute | solution.py:16
  219.7 23.8 %collective-permute-start.7 = (f32[258,1]{1,0:T(8,128)S(1)}, f32[258,1]{1,0:T(8,128)}, u32[]{:S(2)}, u32[]{:S(2)}) collective-permute-start(f32[258,1]{1,0:T(8,128)S(1)} %get-tuple-element.30), channel_id=1, source_target_pairs={{1,0},{2,1},{3,2},{5,4},{6,5},{7,6},{9,8},{10,9},{11,10},{13,12},{... | collective-permute-start | bytes 3104 | tf_op jit(solution)/shard_map/ppermute | solution.py:19
  221.0 0.7 copy-start.12
  221.6 0.6 copy-start.14
  236.4 32.9 %collective-permute-start.24 = (f32[1,4096]{1,0:T(1,128)}, f32[1,4096]{1,0:T(1,128)S(1)}, u32[]{:S(2)}, u32[]{:S(2)}) collective-permute-start(f32[1,4096]{1,0:T(1,128)} %get-tuple-element.53), channel_id=1, source_target_pairs={{0,4},{4,8},{8,12},{12,16},{16,20},{20,24},{24,28},{1,5},{5,9},{9,... | collective-permute-start | bytes 49160 | tf_op jit(solution)/shard_map/ppermute | solution.py:16
  241.5 27.8 %collective-permute-start.25 = (f32[1,4096]{1,0:T(1,128)}, f32[1,4096]{1,0:T(1,128)S(1)}, u32[]{:S(2)}, u32[]{:S(2)}) collective-permute-start(f32[1,4096]{1,0:T(1,128)} %get-tuple-element.52), channel_id=1, source_target_pairs={{4,0},{8,4},{12,8},{16,12},{20,16},{24,20},{28,24},{5,1},{9,5},{13... | collective-permute-start | bytes 49160 | tf_op jit(solution)/shard_map/ppermute | solution.py:19
  261.5 14.5 %copy-start.2 = (f32[256,4096]{1,0:T(8,128)S(1)}, f32[256,4096]{1,0:T(8,128)}, u32[]{:S(2)}) copy-start(f32[256,4096]{1,0:T(8,128)} %add_add_fusion.6) | copy-start | bytes 12582916
  262.6 13.3 %collective-permute-start.8 = (f32[1,4096]{1,0:T(1,128)S(1)}, f32[1,4096]{1,0:T(1,128)S(1)}, u32[]{:S(2)}, u32[]{:S(2)}) collective-permute-start(f32[1,4096]{1,0:T(1,128)S(1)} %get-tuple-element.45), channel_id=1, source_target_pairs={{0,4},{4,8},{8,12},{12,16},{16,20},{20,24},{24,28},{1,5},{5,9},{9,... | collective-permute-start | bytes 49160 | tf_op jit(solution)/shard_map/ppermute | solution.py:16
  267.3 8.6 %collective-permute-start.9 = (f32[1,4096]{1,0:T(1,128)S(1)}, f32[1,4096]{1,0:T(1,128)S(1)}, u32[]{:S(2)}, u32[]{:S(2)}) collective-permute-start(f32[1,4096]{1,0:T(1,128)S(1)} %get-tuple-element.44), channel_id=1, source_target_pairs={{4,0},{8,4},{12,8},{16,12},{20,16},{24,20},{28,24},{5,1},{9,5},{13... | collective-permute-start | bytes 49160 | tf_op jit(solution)/shard_map/ppermute | solution.py:19
  270.4 11.2 %collective-permute-start.26 = (f32[258,1]{1,0:T(8,128)S(1)}, f32[258,1]{1,0:T(8,128)S(1)}, u32[]{:S(2)}, u32[]{:S(2)}) collective-permute-start(f32[258,1]{1,0:T(8,128)S(1)} %get-tuple-element.37), channel_id=1, source_target_pairs={{0,1},{1,2},{2,3},{4,5},{5,6},{6,7},{8,9},{9,10},{10,11},{12,13},{... | collective-permute-start | bytes 3104 | tf_op jit(solution)/shard_map/ppermute | solution.py:16
  274.6 7.6 %collective-permute-start.27 = (f32[258,1]{1,0:T(8,128)S(1)}, f32[258,1]{1,0:T(8,128)}, u32[]{:S(2)}, u32[]{:S(2)}) collective-permute-start(f32[258,1]{1,0:T(8,128)S(1)} %get-tuple-element.36), channel_id=1, source_target_pairs={{1,0},{2,1},{3,2},{5,4},{6,5},{7,6},{9,8},{10,9},{11,10},{13,12},{... | collective-permute-start | bytes 3104 | tf_op jit(solution)/shard_map/ppermute | solution.py:19
  276.0 25.2 %copy-start.16 = (f32[1,4096]{1,0:T(1,128)}, f32[1,4096]{1,0:T(1,128)S(1)}, u32[]{:S(2)}) copy-start(f32[1,4096]{1,0:T(1,128)S(1)} %collective-permute-done.9) | copy-start | bytes 49156
  276.1 34.0 %collective-permute-start.10 = (f32[258,1]{1,0:T(8,128)S(1)}, f32[258,1]{1,0:T(8,128)S(1)}, u32[]{:S(2)}, u32[]{:S(2)}) collective-permute-start(f32[258,1]{1,0:T(8,128)S(1)} %get-tuple-element.29), channel_id=1, source_target_pairs={{0,1},{1,2},{2,3},{4,5},{5,6},{6,7},{8,9},{9,10},{10,11},{12,13},{... | collective-permute-start | bytes 3104 | tf_op jit(solution)/shard_map/ppermute | solution.py:16
  280.1 30.0 %collective-permute-start.11 = (f32[258,1]{1,0:T(8,128)S(1)}, f32[258,1]{1,0:T(8,128)}, u32[]{:S(2)}, u32[]{:S(2)}) collective-permute-start(f32[258,1]{1,0:T(8,128)S(1)} %get-tuple-element.28), channel_id=1, source_target_pairs={{1,0},{2,1},{3,2},{5,4},{6,5},{7,6},{9,8},{10,9},{11,10},{13,12},{... | collective-permute-start | bytes 3104 | tf_op jit(solution)/shard_map/ppermute | solution.py:19
  281.6 0.7 copy-start.13
  302.8 33.4 %collective-permute-start.28 = (f32[1,4096]{1,0:T(1,128)}, f32[1,4096]{1,0:T(1,128)S(1)}, u32[]{:S(2)}, u32[]{:S(2)}) collective-permute-start(f32[1,4096]{1,0:T(1,128)} %get-tuple-element.50), channel_id=1, source_target_pairs={{0,4},{4,8},{8,12},{12,16},{16,20},{20,24},{24,28},{1,5},{5,9},{9,... | collective-permute-start | bytes 49160 | tf_op jit(solution)/shard_map/ppermute | solution.py:16
  308.2 28.0 %collective-permute-start.29 = (f32[1,4096]{1,0:T(1,128)}, f32[1,4096]{1,0:T(1,128)S(1)}, u32[]{:S(2)}, u32[]{:S(2)}) collective-permute-start(f32[1,4096]{1,0:T(1,128)} %get-tuple-element.51), channel_id=1, source_target_pairs={{4,0},{8,4},{12,8},{16,12},{20,16},{24,20},{28,24},{5,1},{9,5},{13... | collective-permute-start | bytes 49160 | tf_op jit(solution)/shard_map/ppermute | solution.py:19
  328.3 14.6 %copy-start.5 = (f32[256,4096]{1,0:T(8,128)S(1)}, f32[256,4096]{1,0:T(8,128)}, u32[]{:S(2)}) copy-start(f32[256,4096]{1,0:T(8,128)} %add_add_fusion.5) | copy-start | bytes 12582916
  329.4 13.4 %collective-permute-start.12 = (f32[1,4096]{1,0:T(1,128)S(1)}, f32[1,4096]{1,0:T(1,128)S(1)}, u32[]{:S(2)}, u32[]{:S(2)}) collective-permute-start(f32[1,4096]{1,0:T(1,128)S(1)} %get-tuple-element.42), channel_id=1, source_target_pairs={{0,4},{4,8},{8,12},{12,16},{16,20},{20,24},{24,28},{1,5},{5,9},{9,... | collective-permute-start | bytes 49160 | tf_op jit(solution)/shard_map/ppermute | solution.py:16
  334.1 16.2 %copy-start.8 = (pred[256,4096]{1,0:T(8,128)(4,1)S(1)}, pred[256,4096]{1,0:T(8,128)(4,1)}, u32[]{:S(2)}) copy-start(pred[256,4096]{1,0:T(8,128)(4,1)} %get-tuple-element.14) | copy-start | bytes 3145732
  334.1 8.8 %collective-permute-start.13 = (f32[1,4096]{1,0:T(1,128)S(1)}, f32[1,4096]{1,0:T(1,128)S(1)}, u32[]{:S(2)}, u32[]{:S(2)}) collective-permute-start(f32[1,4096]{1,0:T(1,128)S(1)} %get-tuple-element.43), channel_id=1, source_target_pairs={{4,0},{8,4},{12,8},{16,12},{20,16},{24,20},{28,24},{5,1},{9,5},{13... | collective-permute-start | bytes 49160 | tf_op jit(solution)/shard_map/ppermute | solution.py:19
  337.3 13.0 %collective-permute-start.30 = (f32[258,1]{1,0:T(8,128)S(1)}, f32[258,1]{1,0:T(8,128)S(1)}, u32[]{:S(2)}, u32[]{:S(2)}) collective-permute-start(f32[258,1]{1,0:T(8,128)S(1)} %get-tuple-element.34), channel_id=1, source_target_pairs={{0,1},{1,2},{2,3},{4,5},{5,6},{6,7},{8,9},{9,10},{10,11},{12,13},{... | collective-permute-start | bytes 3104 | tf_op jit(solution)/shard_map/ppermute | solution.py:16
  341.6 8.7 %collective-permute-start.31 = (f32[258,1]{1,0:T(8,128)S(1)}, f32[258,1]{1,0:T(8,128)S(1)}, u32[]{:S(2)}, u32[]{:S(2)}) collective-permute-start(f32[258,1]{1,0:T(8,128)S(1)} %get-tuple-element.35), channel_id=1, source_target_pairs={{1,0},{2,1},{3,2},{5,4},{6,5},{7,6},{9,8},{10,9},{11,10},{13,12},{... | collective-permute-start | bytes 3104 | tf_op jit(solution)/shard_map/ppermute | solution.py:19
  343.7 27.0 %collective-permute-start.14 = (f32[258,1]{1,0:T(8,128)}, f32[258,1]{1,0:T(8,128)S(1)}, u32[]{:S(2)}, u32[]{:S(2)}) collective-permute-start(f32[258,1]{1,0:T(8,128)} %get-tuple-element.26), channel_id=1, source_target_pairs={{0,1},{1,2},{2,3},{4,5},{5,6},{6,7},{8,9},{9,10},{10,11},{12,13},{... | collective-permute-start | bytes 3104 | tf_op jit(solution)/shard_map/ppermute | solution.py:16
  348.4 22.3 %slice-start.4 = ((s8[8388608]{0:T(1024)(128)(4,1)}), s8[4194304]{0:T(1024)(128)(4,1)S(1)}, s32[]{:S(2)}) async-start(s8[8388608]{0:T(1024)(128)(4,1)} %bitcast.147), calls=%async_computation.6 | async-start | bytes 8388608
  348.4 22.3 %slice-start.5 = ((s8[8388608]{0:T(1024)(128)(4,1)}), s8[4194304]{0:T(1024)(128)(4,1)S(1)}, s32[]{:S(2)}) async-start(s8[8388608]{0:T(1024)(128)(4,1)} %bitcast.147), calls=%async_computation.7 | async-start | bytes 8388608
  348.5 22.3 %copy-start.1 = (f32[256,4096]{1,0:T(8,128)S(1)}, f32[256,4096]{1,0:T(8,128)}, u32[]{:S(2)}) copy-start(f32[256,4096]{1,0:T(8,128)} %copy-done) | copy-start | bytes 12582916
  348.5 22.3 %copy-start.3 = (bf16[1,4,64,4096]{3,2,1,0:T(8,128)(2,1)S(1)}, bf16[1,4,64,4096]{3,2,1,0:T(8,128)(2,1)}, u32[]{:S(2)}) copy-start(bf16[1,4,64,4096]{3,2,1,0:T(8,128)(2,1)} %get-tuple-element.48) | copy-start | bytes 6291460
  348.5 22.2 %collective-permute-start.15 = (f32[258,1]{1,0:T(8,128)}, f32[258,1]{1,0:T(8,128)S(1)}, u32[]{:S(2)}, u32[]{:S(2)}) collective-permute-start(f32[258,1]{1,0:T(8,128)} %get-tuple-element.27), channel_id=1, source_target_pairs={{1,0},{2,1},{3,2},{5,4},{6,5},{7,6},{9,8},{10,9},{11,10},{13,12},{... | collective-permute-start | bytes 3104 | tf_op jit(solution)/shard_map/ppermute | solution.py:19
  370.7 21.2 %copy-start.9 = (f32[1,256,4096]{2,1,0:T(8,128)S(1)}, f32[1,256,4096]{2,1,0:T(8,128)}, u32[]{:S(2)}) copy-start(f32[1,256,4096]{2,1,0:T(8,128)} %get-tuple-element.11) | copy-start | bytes 12582916
  398.3 189.9 %all-to-all-start.1 = ((f32[4,2,64,4096]{3,2,1,0:T(8,128)}), f32[4,2,64,4096]{3,2,1,0:T(8,128)}, u32[]{:S(2)}, u32[]{:S(2)}) async-start(f32[4,2,64,4096]{3,2,1,0:T(8,128)} %pad_maximum_fusion), calls=%async_computation.1 | async-start | bytes 16777216 | tf_op jit(solution)/shard_map/all_to_all | solution.py:77
